TPU v7x, 512 devices: a whole 4x4x16 slice. The times are simulated.
512 devices in a mesh: box: 128 (over z, y, core), level: 4 (over x).
Axes of the slice: x: 4, y: 4, z: 16, core: 2. Of those that a mesh axis runs over, the one named last changes fastest.
Arguments:
- rhs_field: float32 [4, 2048, 128], P(None, 'box'), may hold values from -6 to 6
- self_coef: float32 [2048, 128], P('box'), may hold values from 2 to 4
- expand: bfloat16 [2048, 256, 128], P('box'), may hold values from -0.5 to 0.5
- near_ops: bfloat16 [26, 128, 128], replicated, may hold values from -0.109375 to 0.109375
- class_ops: bfloat16 [128, 256, 256], P('box', 'level'), may hold values from -0.046875 to 0.046875
- near_src: int32 [2048, 26], P('box'), may hold values from 0 to 47
- send_rows: int32 [128, 128, 2], P('box'), may hold values from 0 to 15
- list_slot: int32 [2048, 64], P('box'), may hold values from 0 to 255
- list_class: int32 [2048, 64], P('box'), may hold values from 0 to 127, all different within a row
Outputs:
- solution: float32 [4, 2048, 128], P(None, 'box')
Inputs may be any that keep to these rules, and one draw needn't show every extreme that they name: `near_src`: the near-field neighbours of a box lie among the boxes of the index of box before it, its own and the one after it, counted in that order. `send_rows`: each entry is a box of the sending index. `list_slot`: entry q * 2 + j names the j-th row sent by index q of box. `list_class`: the classes of one box's list are distinct.
All inputs are finite; a program needn't handle non-finite values.
Results may differ from a plain program's by a relative error of at most 0.004.
Values may be sent and summed in bfloat16 or wider, within the bound.
A program may use at most 64 MiB of HBM per device.

v0:
```python
import math
import jax
import jax.numpy as jnp
from jax import lax
from jax.sharding import PartitionSpec as P


def extended_2(block, sides, width):
    for axis, dim in sides:
        count = lax.axis_size(axis)
        forward = [(i, i + 1) for i in range(count - 1)]
        backward = [(target, source) for source, target in forward]
        low = lax.ppermute(
            lax.slice_in_dim(block, block.shape[dim] - width, None, axis=dim), axis, forward
        )
        high = lax.ppermute(lax.slice_in_dim(block, 0, width, axis=dim), axis, backward)
        block = jnp.concatenate([low, block, high], axis=dim)
    return block


def slot_table(list_slot, list_class, classes):
    labels = jnp.arange(classes, dtype=jnp.int32)
    matches = list_class[:, :, None] == labels[None, None, :]
    return jnp.sum(jnp.where(matches, list_slot[:, :, None] + 1, 0), axis=1) - 1


def apply_classes(totals, operators, offset, table, received):
    count = operators.shape[0]
    picked = lax.dynamic_slice_in_dim(table, offset, count, 1)
    sources = jnp.where(
        (picked >= 0)[:, :, None, None],
        received[jnp.maximum(picked, 0)],
        jnp.zeros((), received.dtype),
    )
    return totals + jnp.einsum(
        "cqp,tcrp->trq", operators, sources, preferred_element_type=jnp.float32
    )


def fold_classes(totals, pieces, offset, table, received):
    count = pieces.shape[0]
    stride = math.gcd(count, 16)

    def step_once(number, current):
        operators = lax.dynamic_slice_in_dim(pieces, number * stride, stride, 0)
        return apply_classes(current, operators, offset + number * stride, table, received)

    return lax.fori_loop(0, count // stride, step_once, totals)


def inner(first, second):
    return jnp.sum(first * second, axis=(1, 2))


def spread(values, field):
    return values[:, None, None] * field


def per_device(
    rhs_field, self_coef, expand, near_ops, class_ops, near_src, send_rows, list_slot, list_class
):
    boxes = expand.shape[0]
    band = class_ops.shape[1]
    classes = class_ops.shape[0] * lax.axis_size("box")
    table = slot_table(list_slot, list_class, classes)
    level_index = lax.axis_index("level")
    cached = lax.all_gather(class_ops, "box", axis=0, tiled=True)

    def apply_matrix(field):
        field_half = field.astype(jnp.bfloat16)
        multipoles = jnp.einsum(
            "tpk,rtk->trp", expand, field_half, preferred_element_type=jnp.float32
        ).astype(jnp.bfloat16)
        outgoing = multipoles[send_rows[0]]
        received = lax.all_to_all(outgoing, "box", split_axis=0, concat_axis=0, tiled=True)
        received = received.reshape((-1,) + received.shape[2:])
        extended = extended_2(field_half, (("box", 1),), boxes)
        neighbours = extended[:, near_src]
        near_part = jnp.einsum(
            "kij,rtkj->rti", near_ops, neighbours, preferred_element_type=jnp.float32
        )
        empty = jnp.zeros((boxes, field.shape[0], band), jnp.float32)
        local_full = fold_classes(empty, cached, 0, table, received)
        local_half = local_full.astype(jnp.bfloat16)
        expand_rows = lax.dynamic_slice_in_dim(expand, level_index * band, band, 1)
        partial_field = jnp.einsum(
            "tqk,trq->rtk", expand_rows, local_half, preferred_element_type=jnp.float32
        )
        far_part = lax.psum(partial_field.astype(jnp.bfloat16), "level").astype(jnp.float32)
        return self_coef[None] * field + near_part + far_part

    def totals(*pairs):
        stacked = jnp.stack([inner(a, b) for a, b in pairs])
        return jnp.sum(lax.all_gather(stacked, "box"), axis=0)

    first_image = apply_matrix(rhs_field)
    rr, ra = totals((rhs_field, rhs_field), (rhs_field, first_image))
    h_one_one = ra / rr
    second = first_image - spread(h_one_one, rhs_field)
    second_image = apply_matrix(second)
    uu, rb, ub, bb = totals(
        (second, second),
        (rhs_field, second_image),
        (second, second_image),
        (second_image, second_image),
    )
    beta = jnp.sqrt(rr)
    length = jnp.sqrt(uu)
    h_two_one = length / beta
    h_one_two = rb / (beta * length)
    h_two_two = ub / uu
    gram_aa = h_one_one * h_one_one + h_two_one * h_two_one
    gram_ab = h_one_one * h_one_two + h_two_one * h_two_two
    gram_bb = bb / uu
    right_a = beta * h_one_one
    right_b = beta * h_one_two
    determinant = gram_aa * gram_bb - gram_ab * gram_ab
    coef_a = (gram_bb * right_a - gram_ab * right_b) / determinant
    coef_b = (gram_aa * right_b - gram_ab * right_a) / determinant
    return spread(coef_a / beta, rhs_field) + spread(coef_b / length, second)


def solution(mesh):
    return jax.shard_map(
        per_device,
        mesh=mesh,
        in_specs=(
            P(None, "box", None),
            P("box", None),
            P("box", None, None),
            P(),
            P("box", "level", None),
            P("box", None),
            P("box", None, None),
            P("box", None),
            P("box", None),
        ),
        out_specs=P(None, "box", None),
        check_vma=False,
    )
```

profile of v0, /device:TPU:1, one launch (start us, length us, event | category | flops | bytes accessed | tf_op | source)
XLA Modules:
  0.0 477.1 jit_solution(12812204908708037069)
XLA Ops:
  9.4 1.9 gather_fusion.3
  11.3 20.6 %all-to-all-start = ((bf16[128,2,4,256]{3,2,1,0:T(4,128)(2,1)}), bf16[128,2,4,256]{3,2,1,0:T(4,128)(2,1)S(1)}, u32[]{:S(2)}, u32[]{:S(2)}) async-start(bf16[128,2,4,256]{3,2,1,0:T(4,128)(2,1)} %bitcast.6), calls=%async_computation | async-start | bytes 1048576 | tf_op jit(solution)/shard_map/all_to_all | solution.py:75
  31.9 2.8 collective-permute-start.1
  34.7 2.8 collective-permute-start
  40.1 2.2 gather_fusion.2
  42.3 21.9 %all-to-all-done = bf16[128,2,4,256]{3,2,1,0:T(4,128)(2,1)S(1)} async-done(((bf16[128,2,4,256]{3,2,1,0:T(4,128)(2,1)}), bf16[128,2,4,256]{3,2,1,0:T(4,128)(2,1)S(1)}, u32[]{:S(2)}, u32[]{:S(2)}) %all-to-all-start) | async-done | bytes 524320 | tf_op jit(solution)/shard_map/all_to_all | solution.py:75
  64.2 96.6 %all-gather.6.cloned.1.call-done = bf16[128,64,256]{2,1,0:T(8,128)(2,1)} async-done(((bf16[1,64,256]{2,1,0:T(8,128)(2,1)}), bf16[128,64,256]{2,1,0:T(8,128)(2,1)}) %all-gather.6.cloned.1.call-update) | async-done | bytes 4194320 | tf_op jit(solution)/shard_map/all_gather | solution.py:67
  160.8 24.6 %while.28 = (s32[]{:T(128)}, f32[16,4,64]{2,0,1:T(8,128)S(1)}, s32[16,128]{1,0:T(8,128)S(1)}, bf16[256,4,256]{2,1,0:T(4,128)(2,1)S(1)}, bf16[128,64,256]{2,1,0:T...) while((s32[]{:T(128)}, f32[16,4,64]{2,0,1:T(8,128)S(1)}, ...), condition=%wide.region_2.3_spmd.clone, body=%wide.region_1.2_spmd.clone.sunk | while | flops 33826312 | bytes 2142377 | solution.py:48
  161.0 1.2 gather_fusion
  162.3 1.5 fusion.51
  164.1 1.2 gather_fusion
  165.4 1.5 fusion.51
  167.1 1.2 gather_fusion
  168.5 1.5 fusion.51
  170.2 1.2 gather_fusion
  171.5 1.5 fusion.51
  173.3 1.2 gather_fusion
  174.6 1.5 fusion.51
  176.4 1.2 gather_fusion
  177.7 1.5 fusion.51
  179.4 1.2 gather_fusion
  180.8 1.5 fusion.51
  182.5 1.2 gather_fusion
  183.8 1.5 fusion.51
  185.6 13.1 %psum.14 = bf16[4,16,128]{2,1,0:T(8,128)(2,1)S(1)} all-reduce(bf16[4,16,128]{2,1,0:T(8,128)(2,1)S(1)} %bitcast.147), channel_id=1, replica_groups=mesh['box'=128,'level'=4] {'level'}, use_global_device_ids=true, to_apply=%region_3.4 | all-reduce | flops 8192 | bytes 32768 | tf_op jit(solution)/shard_map/psum | solution.py:89
  199.2 84.8 %all-gather.2 = f32[128,2,4]{2,1,0:T(2,128)S(1)} all-gather(f32[1,2,4]{2,1,0:T(2,128)S(1)} %maximum_bitcast_fusion.1), channel_id=2, replica_groups=mesh['box'=128,'level'=4] {'box'}, dimensions={0}, use_global_device_ids=true | all-gather | bytes 4128 | tf_op jit(solution)/shard_map/all_gather | solution.py:94
  284.7 1.9 gather_fusion.5
  286.6 10.3 %all-to-all-start.1 = ((bf16[128,2,4,256]{3,2,1,0:T(4,128)(2,1)}), bf16[128,2,4,256]{3,2,1,0:T(4,128)(2,1)S(1)}, u32[]{:S(2)}, u32[]{:S(2)}) async-start(bf16[128,2,4,256]{3,2,1,0:T(4,128)(2,1)} %bitcast.18), calls=%async_computation.1 | async-start | bytes 1048576 | tf_op jit(solution)/shard_map/all_to_all | solution.py:75
  296.9 2.8 collective-permute-start.3
  299.7 2.9 collective-permute-start.2
  303.4 2.2 gather_fusion.4
  305.6 22.2 %all-to-all-done.1 = bf16[128,2,4,256]{3,2,1,0:T(4,128)(2,1)S(1)} async-done(((bf16[128,2,4,256]{3,2,1,0:T(4,128)(2,1)}), bf16[128,2,4,256]{3,2,1,0:T(4,128)(2,1)S(1)}, u32[]{:S(2)}, u32[]{:S(2)}) %all-to-all-start.1) | async-done | bytes 524320 | tf_op jit(solution)/shard_map/all_to_all | solution.py:75
  327.7 24.5 %while.29 = (s32[]{:T(128)}, f32[16,4,64]{2,0,1:T(8,128)S(1)}, s32[16,128]{1,0:T(8,128)S(1)}, bf16[256,4,256]{2,1,0:T(4,128)(2,1)S(1)}, bf16[128,64,256]{2,1,0:T...) while((s32[]{:T(128)}, f32[16,4,64]{2,0,1:T(8,128)S(1)}, ...), condition=%wide.region_9.10_spmd.clone, body=%wide.region_8.9_spmd.clone.sunk | while | flops 33826312 | bytes 2142377 | solution.py:48
  329.2 1.5 fusion.53
  331.0 1.2 gather_fusion.1
  332.3 1.5 fusion.53
  334.0 1.2 gather_fusion.1
  335.4 1.5 fusion.53
  337.1 1.2 gather_fusion.1
  338.4 1.5 fusion.53
  340.2 1.2 gather_fusion.1
  341.5 1.5 fusion.53
  344.5 1.5 fusion.53
  347.6 1.5 fusion.53
  349.3 1.2 gather_fusion.1
  350.7 1.5 fusion.53
  352.4 10.8 %psum.15 = bf16[4,16,128]{2,1,0:T(8,128)(2,1)S(1)} all-reduce(bf16[4,16,128]{2,1,0:T(8,128)(2,1)S(1)} %bitcast.148), channel_id=1, replica_groups=mesh['box'=128,'level'=4] {'level'}, use_global_device_ids=true, to_apply=%region_10.11 | all-reduce | flops 8192 | bytes 32768 | tf_op jit(solution)/shard_map/psum | solution.py:89
  363.8 105.6 %all-gather.3 = f32[128,4,4]{2,1,0:T(4,128)S(1)} all-gather(f32[1,4,4]{2,1,0:T(4,128)S(1)} %maximum_bitcast_fusion), channel_id=3, replica_groups=mesh['box'=128,'level'=4] {'box'}, dimensions={0}, use_global_device_ids=true | all-gather | bytes 8256 | tf_op jit(solution)/shard_map/all_gather | solution.py:94
  (132 shorter events, 17.9 us)
Async XLA Ops:
  6.5 2.5 copy-start
  6.5 154.3 %all-gather.6.cloned.1.call-start = ((), (), s32[]{:S(2)}) async-start(), calls=%async_computation.2 | async-start | bytes 4227072 | tf_op jit(solution)/shard_map/all_gather | solution.py:67
  11.3 52.9 %all-to-all-start = ((bf16[128,2,4,256]{3,2,1,0:T(4,128)(2,1)}), bf16[128,2,4,256]{3,2,1,0:T(4,128)(2,1)S(1)}, u32[]{:S(2)}, u32[]{:S(2)}) async-start(bf16[128,2,4,256]{3,2,1,0:T(4,128)(2,1)} %bitcast.6), calls=%async_computation | async-start | bytes 1048576 | tf_op jit(solution)/shard_map/all_to_all | solution.py:75
  31.9 8.2 %collective-permute-start.1 = (bf16[4,16,128]{2,0,1:T(4,128)(2,1)S(1)}, bf16[4,16,128]{2,0,1:T(4,128)(2,1)S(1)}, u32[]{:S(2)}, u32[]{:S(2)}) collective-permute-start(bf16[4,16,128]{2,0,1:T(4,128)(2,1)S(1)} %copy.87), channel_id=1, source_target_pairs={{4,0},{8,4},{12,8},{16,12},{20,16},{24,20},{28,24},{32,28},{36,32}... | collective-permute-start | bytes 49160 | tf_op jit(solution)/shard_map/ppermute | solution.py:16
  34.7 5.4 %collective-permute-start = (bf16[4,16,128]{2,0,1:T(4,128)(2,1)S(1)}, bf16[4,16,128]{2,0,1:T(4,128)(2,1)S(1)}, u32[]{:S(2)}, u32[]{:S(2)}) collective-permute-start(bf16[4,16,128]{2,0,1:T(4,128)(2,1)S(1)} %copy.87), channel_id=1, source_target_pairs={{0,4},{4,8},{8,12},{12,16},{16,20},{20,24},{24,28},{28,32},{32,36}... | collective-permute-start | bytes 49160 | tf_op jit(solution)/shard_map/ppermute | solution.py:13
  160.8 37.9 %copy-start.1 = (bf16[26,128,128]{2,1,0:T(8,128)(2,1)S(1)}, bf16[26,128,128]{2,1,0:T(8,128)(2,1)}, u32[]{:S(2)}) copy-start(bf16[26,128,128]{2,1,0:T(8,128)(2,1)} %param.16) | copy-start | bytes 2555908
  160.8 37.9 %copy-start.2 = (f32[4,16,128]{2,1,0:T(8,128)S(1)}, f32[4,16,128]{2,1,0:T(8,128)}, u32[]{:S(2)}) copy-start(f32[4,16,128]{2,1,0:T(8,128)} %param.13) | copy-start | bytes 98308
  160.8 37.9 %copy-start.3 = (f32[16,128]{1,0:T(8,128)S(1)}, f32[16,128]{1,0:T(8,128)}, u32[]{:S(2)}) copy-start(f32[16,128]{1,0:T(8,128)} %param.14) | copy-start | bytes 24580
  286.6 41.2 %all-to-all-start.1 = ((bf16[128,2,4,256]{3,2,1,0:T(4,128)(2,1)}), bf16[128,2,4,256]{3,2,1,0:T(4,128)(2,1)S(1)}, u32[]{:S(2)}, u32[]{:S(2)}) async-start(bf16[128,2,4,256]{3,2,1,0:T(4,128)(2,1)} %bitcast.18), calls=%async_computation.1 | async-start | bytes 1048576 | tf_op jit(solution)/shard_map/all_to_all | solution.py:75
  296.9 5.8 %collective-permute-start.3 = (bf16[4,16,128]{2,1,0:T(8,128)(2,1)S(1)}, bf16[4,16,128]{2,1,0:T(8,128)(2,1)S(1)}, u32[]{:S(2)}, u32[]{:S(2)}) collective-permute-start(bf16[4,16,128]{2,1,0:T(8,128)(2,1)S(1)} %get-tuple-element.261), channel_id=1, source_target_pairs={{4,0},{8,4},{12,8},{16,12},{20,16},{24,20},{28,24},{32,28},{36,32}... | collective-permute-start | bytes 49160 | tf_op jit(solution)/shard_map/ppermute | solution.py:16
  299.7 3.6 collective-permute-start.2
Sparse Core Ops, SparseCore 0:
  10.5 150.2 all-gather.5
where the time goes:
time: 478 us; the launch traced here: 477 us
  blocking collectives  214 us (45%)
  waiting for transfers between devices  142 us (30%)
  starting transfers between devices  42.2 us (9%)
  local copies, waits for them, and re-layouts  30.7 us (6%)
  matrix products  26.8 us (6%)
  between operations  13.6 us (3%)
  other arithmetic  6.97 us (1%)
    all_gather x2, blocking collectives, totals(): return jnp.sum(lax.all_gather(stacked, 'box'), axis=0)  190 us
    all_gather x1, waiting for transfers between devices, per_device(): cached = lax.all_gather(class_ops, 'box', axis=0, tiled=True)  96.6 us
    all_to_all x2, waiting for transfers between devices, apply_matrix(): lax.all_to_all(outgoing, 'box', split_axis=0, concat_axis=0, tiled=True)  44.1 us
    all_to_all x2, starting transfers between devices, apply_matrix(): lax.all_to_all(outgoing, 'box', split_axis=0, concat_axis=0, tiled=True)  30.9 us
    dot_general x16, matrix products, apply_classes(): jnp.einsum('cqp,tcrp->trq', operators, sources, preferred_element_type=jn...  24.6 us
    psum x2, blocking collectives, apply_matrix(): lax.psum(partial_field.astype(jnp.bfloat16), 'level').astype(jnp.float32)  23.9 us
    gather x16, local copies, waits for them, and re-layouts, apply_classes(): received[jnp.maximum(picked, 0)]  18.5 us
  transfers between devices with their start and end apart: 7, of which 4 were waited for; matrix products, arithmetic and copies ran while one was open for 2% of the time, Pallas kernels for 0%

commit v1 on v0

--- a/solution.py
+++ b/solution.py
@@ -3,6 +3,10 @@
 import jax.numpy as jnp
 from jax import lax
 from jax.sharding import PartitionSpec as P
+
+change_slots = lambda a0: jnp.concatenate(
+    jax.lax.all_to_all(jnp.stack(jax.lax.axis_size("box") * [a0], axis=0), "box", 0, 0), axis=0
+)
 
 
 def extended_2(block, sides, width):
@@ -64,7 +68,7 @@
     classes = class_ops.shape[0] * lax.axis_size("box")
     table = slot_table(list_slot, list_class, classes)
     level_index = lax.axis_index("level")
-    cached = lax.all_gather(class_ops, "box", axis=0, tiled=True)
+    cached = change_slots(class_ops)
 
     def apply_matrix(field):
         field_half = field.astype(jnp.bfloat16)

time: 478 us -> 567 us (1.19)
  blocking collectives: 214 us -> 271 us
  waiting for transfers between devices: 142 us -> 198 us
  between operations: 13.6 us -> 0.28 us
  starting transfers between devices: 42.2 us -> 30.8 us
    all_to_all x0 -> x1, waiting for transfers between devices: none -> 172 us  [jax.lax.all_to_all(jnp.stack(jax.lax.axis_size('box') * [a0], axis=0), 'b...]
    all_gather x1 -> x0, waiting for transfers between devices: 96.6 us -> none  [per_device(): cached = lax.all_gather(class_ops, 'box', axis=0, tiled=True)]
    all_to_all x0 -> x1, blocking collectives: none -> 51.2 us  [apply_matrix(): lax.all_to_all(outgoing, 'box', split_axis=0, concat_axis=0, tiled=True)]
    all_to_all x2 -> x1, waiting for transfers between devices: 44.1 us -> 19.7 us  [apply_matrix(): lax.all_to_all(outgoing, 'box', split_axis=0, concat_axis=0, tiled=True)]
    all_to_all x2 -> x1, starting transfers between devices: 30.9 us -> 10.2 us  [apply_matrix(): lax.all_to_all(outgoing, 'box', split_axis=0, concat_axis=0, tiled=True)]
    all_to_all x0 -> x1, starting transfers between devices: none -> 9.7 us  [jax.lax.all_to_all(jnp.stack(jax.lax.axis_size('box') * [a0], axis=0), 'b...]
    ppermute x2, waiting for transfers between devices: 0.01 us -> 6.56 us  [extended_2(): lax.ppermute(lax.slice_in_dim(block, 0, width, axis=dim), axis, backward)]
    all_gather x2, blocking collectives: 190 us -> 196 us  [totals(): return jnp.sum(lax.all_gather(stacked, 'box'), axis=0)]
  transfers between devices with their start and end apart: 7 -> 6, of which waited for: 4 -> 4; matrix products, arithmetic and copies ran while one was open for 2% -> 1% of each run, Pallas kernels for 0% -> 0%
where the time goes in v1:
time: 567 us; the launch traced here: 566 us
  blocking collectives  271 us (48%)
  waiting for transfers between devices  198 us (35%)
  local copies, waits for them, and re-layouts  33.2 us (6%)
  starting transfers between devices  30.8 us (5%)
  matrix products  26.7 us (5%)
    all_gather x2, blocking collectives, totals(): return jnp.sum(lax.all_gather(stacked, 'box'), axis=0)  196 us
    all_to_all x1, waiting for transfers between devices, jax.lax.all_to_all(jnp.stack(jax.lax.axis_size('box') * [a0], axis=0), 'b...  172 us
    all_to_all x1, blocking collectives, apply_matrix(): lax.all_to_all(outgoing, 'box', split_axis=0, concat_axis=0, tiled=True)  51.2 us
    dot_general x16, matrix products, apply_classes(): jnp.einsum('cqp,tcrp->trq', operators, sources, preferred_element_type=jn...  24.5 us
    psum x2, blocking collectives, apply_matrix(): lax.psum(partial_field.astype(jnp.bfloat16), 'level').astype(jnp.float32)  24 us
    all_to_all x1, waiting for transfers between devices, apply_matrix(): lax.all_to_all(outgoing, 'box', split_axis=0, concat_axis=0, tiled=True)  19.7 us
    gather x16, local copies, waits for them, and re-layouts, apply_classes(): received[jnp.maximum(picked, 0)]  18.5 us
  transfers between devices with their start and end apart: 6, of which 4 were waited for; matrix products, arithmetic and copies ran while one was open for 1% of the time, Pallas kernels for 0%

profile of v1, /device:TPU:1, one launch (start us, length us, event | category | flops | bytes accessed | tf_op | source)
XLA Modules:
  0.0 566.0 jit_solution(11493455042842846594)
XLA Ops:
  2.2 1.2 gather_fusion.3
  3.4 51.2 %all_to_all.15 = bf16[128,2,4,256]{3,2,1,0:T(4,128)(2,1)S(1)} all-to-all(bf16[128,2,4,256]{3,2,1,0:T(4,128)(2,1)S(1)} %bitcast.149), channel_id=1, replica_groups=mesh['box'=128,'level'=4] {'box'}, dimensions={0} | all-to-all | bytes 1048576 | tf_op jit(solution)/shard_map/all_to_all | solution.py:79
  54.6 3.2 stack.18
  57.8 9.7 %all-to-all-start.1 = ((bf16[128,1,64,256]{3,2,1,0:T(8,128)(2,1)}), bf16[128,1,64,256]{3,2,1,0:T(8,128)(2,1)}, u32[]{:S(2)}, u32[]{:S(2)}) async-start(bf16[128,1,64,256]{3,2,1,0:T(8,128)(2,1)} %stack.18), calls=%async_computation.1 | async-start | bytes 8388608 | tf_op jit(solution)/shard_map/all_to_all | solution.py:8
  67.5 3.5 collective-permute-start
  71.1 1.9 collective-permute-start.1
  73.5 3.1 collective-permute-done.1
  76.7 2.2 gather_fusion.2
  78.9 172.1 %all-to-all-done.1 = bf16[128,1,64,256]{3,2,1,0:T(8,128)(2,1)} async-done(((bf16[128,1,64,256]{3,2,1,0:T(8,128)(2,1)}), bf16[128,1,64,256]{3,2,1,0:T(8,128)(2,1)}, u32[]{:S(2)}, u32[]{:S(2)}) %all-to-all-start.1) | async-done | bytes 4194336 | tf_op jit(solution)/shard_map/all_to_all | solution.py:8
  251.0 24.4 %while.28 = (s32[]{:T(128)}, f32[16,4,64]{2,0,1:T(8,128)S(1)}, s32[16,128]{1,0:T(8,128)S(1)}, bf16[256,4,256]{2,1,0:T(4,128)(2,1)S(1)}, bf16[128,64,256]{2,1,0:T...) while((s32[]{:T(128)}, f32[16,4,64]{2,0,1:T(8,128)S(1)}, ...), condition=%wide.region_2.3_spmd.clone, body=%wide.region_1.2_spmd.clone.sunk | while | flops 33826312 | bytes 2142369 | solution.py:52
  252.5 1.5 fusion.51
  254.3 1.2 gather_fusion
  255.6 1.5 fusion.51
  257.3 1.2 gather_fusion
  258.7 1.5 fusion.51
  260.4 1.2 gather_fusion
  261.7 1.5 fusion.51
  263.4 1.2 gather_fusion
  264.8 1.5 fusion.51
  266.5 1.2 gather_fusion
  267.8 1.5 fusion.51
  269.5 1.2 gather_fusion
  270.9 1.5 fusion.51
  273.9 1.5 fusion.51
  275.7 13.1 %psum.14 = bf16[4,16,128]{2,1,0:T(8,128)(2,1)S(1)} all-reduce(bf16[4,16,128]{2,1,0:T(8,128)(2,1)S(1)} %bitcast.150), channel_id=1, replica_groups=mesh['box'=128,'level'=4] {'level'}, use_global_device_ids=true, to_apply=%region_3.4 | all-reduce | flops 8192 | bytes 32768 | tf_op jit(solution)/shard_map/psum | solution.py:93
  289.4 90.5 %all-gather.2 = f32[128,2,4]{2,1,0:T(2,128)S(1)} all-gather(f32[1,2,4]{2,1,0:T(2,128)S(1)} %maximum_bitcast_fusion.1), channel_id=2, replica_groups=mesh['box'=128,'level'=4] {'box'}, dimensions={0}, use_global_device_ids=true | all-gather | bytes 4128 | tf_op jit(solution)/shard_map/all_gather | solution.py:98
  380.5 1.9 gather_fusion.5
  382.4 10.2 %all-to-all-start.2 = ((bf16[128,2,4,256]{3,2,1,0:T(4,128)(2,1)}), bf16[128,2,4,256]{3,2,1,0:T(4,128)(2,1)S(1)}, u32[]{:S(2)}, u32[]{:S(2)}) async-start(bf16[128,2,4,256]{3,2,1,0:T(4,128)(2,1)} %bitcast.20), calls=%async_computation.2 | async-start | bytes 1048576 | tf_op jit(solution)/shard_map/all_to_all | solution.py:79
  392.7 3.5 collective-permute-start.2
  396.2 1.9 collective-permute-start.3
  398.2 3.4 collective-permute-done.3
  401.6 2.2 gather_fusion.4
  403.8 19.7 %all-to-all-done.2 = bf16[128,2,4,256]{3,2,1,0:T(4,128)(2,1)S(1)} async-done(((bf16[128,2,4,256]{3,2,1,0:T(4,128)(2,1)}), bf16[128,2,4,256]{3,2,1,0:T(4,128)(2,1)S(1)}, u32[]{:S(2)}, u32[]{:S(2)}) %all-to-all-start.2) | async-done | bytes 524320 | tf_op jit(solution)/shard_map/all_to_all | solution.py:79
  423.5 24.4 %while.29 = (s32[]{:T(128)}, f32[16,4,64]{2,0,1:T(8,128)S(1)}, s32[16,128]{1,0:T(8,128)S(1)}, bf16[256,4,256]{2,1,0:T(4,128)(2,1)S(1)}, bf16[128,64,256]{2,1,0:T...) while((s32[]{:T(128)}, f32[16,4,64]{2,0,1:T(8,128)S(1)}, ...), condition=%wide.region_9.10_spmd.clone, body=%wide.region_8.9_spmd.clone.sunk | while | flops 33826312 | bytes 2142369 | solution.py:52
  425.0 1.5 fusion.53
  426.7 1.2 gather_fusion.1
  428.0 1.5 fusion.53
  429.8 1.2 gather_fusion.1
  431.1 1.5 fusion.53
  434.2 1.5 fusion.53
  437.2 1.5 fusion.53
  438.9 1.2 gather_fusion.1
  440.3 1.5 fusion.53
  442.0 1.2 gather_fusion.1
  443.3 1.5 fusion.53
  446.4 1.5 fusion.53
  448.1 10.8 %psum.15 = bf16[4,16,128]{2,1,0:T(8,128)(2,1)S(1)} all-reduce(bf16[4,16,128]{2,1,0:T(8,128)(2,1)S(1)} %bitcast.151), channel_id=1, replica_groups=mesh['box'=128,'level'=4] {'level'}, use_global_device_ids=true, to_apply=%region_10.11 | all-reduce | flops 8192 | bytes 32768 | tf_op jit(solution)/shard_map/psum | solution.py:93
  459.5 105.6 %all-gather.3 = f32[128,4,4]{2,1,0:T(4,128)S(1)} all-gather(f32[1,4,4]{2,1,0:T(4,128)S(1)} %maximum_bitcast_fusion), channel_id=3, replica_groups=mesh['box'=128,'level'=4] {'box'}, dimensions={0}, use_global_device_ids=true | all-gather | bytes 8256 | tf_op jit(solution)/shard_map/all_gather | solution.py:98
  (137 shorter events, 18.0 us)
Async XLA Ops:
  0.0 1.8 copy-start
  57.8 15.2 %copy-start.5 = (s32[16,26]{1,0:T(8,128)S(1)}, s32[16,26]{1,0:T(8,128)}, u32[]{:S(2)}) copy-start(s32[16,26]{1,0:T(8,128)} %param.18) | copy-start | bytes 4996
  57.8 15.3 %copy-start.6 = (s32[16,64]{1,0:T(8,128)S(1)}, s32[16,64]{1,0:T(8,128)}, u32[]{:S(2)}) copy-start(s32[16,64]{1,0:T(8,128)} %param.20) | copy-start | bytes 12292
  57.8 15.3 %copy-start.4 = (s32[16,64]{1,0:T(8,128)S(1)}, s32[16,64]{1,0:T(8,128)}, u32[]{:S(2)}) copy-start(s32[16,64]{1,0:T(8,128)} %param.21) | copy-start | bytes 12292
  57.8 193.2 %all-to-all-start.1 = ((bf16[128,1,64,256]{3,2,1,0:T(8,128)(2,1)}), bf16[128,1,64,256]{3,2,1,0:T(8,128)(2,1)}, u32[]{:S(2)}, u32[]{:S(2)}) async-start(bf16[128,1,64,256]{3,2,1,0:T(8,128)(2,1)} %stack.18), calls=%async_computation.1 | async-start | bytes 8388608 | tf_op jit(solution)/shard_map/all_to_all | solution.py:8
  67.5 6.0 %collective-permute-start = (bf16[4,16,128]{2,0,1:T(4,128)(2,1)S(1)}, bf16[4,16,128]{2,0,1:T(4,128)(2,1)S(1)}, u32[]{:S(2)}, u32[]{:S(2)}) collective-permute-start(bf16[4,16,128]{2,0,1:T(4,128)(2,1)S(1)} %copy.87), channel_id=1, source_target_pairs={{0,4},{4,8},{8,12},{12,16},{16,20},{20,24},{24,28},{28,32},{32,36}... | collective-permute-start | bytes 49160 | tf_op jit(solution)/shard_map/ppermute | solution.py:17
  71.1 5.6 collective-permute-start.1
  251.0 37.8 %copy-start.1 = (bf16[26,128,128]{2,1,0:T(8,128)(2,1)S(1)}, bf16[26,128,128]{2,1,0:T(8,128)(2,1)}, u32[]{:S(2)}) copy-start(bf16[26,128,128]{2,1,0:T(8,128)(2,1)} %param.16) | copy-start | bytes 2555908
  251.0 37.8 %copy-start.2 = (f32[4,16,128]{2,1,0:T(8,128)S(1)}, f32[4,16,128]{2,1,0:T(8,128)}, u32[]{:S(2)}) copy-start(f32[4,16,128]{2,1,0:T(8,128)} %param.13) | copy-start | bytes 98308
  251.0 37.8 %copy-start.3 = (f32[16,128]{1,0:T(8,128)S(1)}, f32[16,128]{1,0:T(8,128)}, u32[]{:S(2)}) copy-start(f32[16,128]{1,0:T(8,128)} %param.14) | copy-start | bytes 24580
  382.4 41.1 %all-to-all-start.2 = ((bf16[128,2,4,256]{3,2,1,0:T(4,128)(2,1)}), bf16[128,2,4,256]{3,2,1,0:T(4,128)(2,1)S(1)}, u32[]{:S(2)}, u32[]{:S(2)}) async-start(bf16[128,2,4,256]{3,2,1,0:T(4,128)(2,1)} %bitcast.20), calls=%async_computation.2 | async-start | bytes 1048576 | tf_op jit(solution)/shard_map/all_to_all | solution.py:79
  392.7 5.5 collective-permute-start.2
  396.2 5.4 collective-permute-start.3
